TPU v7x, 128 devices: a whole 4x4x4 slice. The times are simulated.
128 devices in a mesh: comp: 16 (over x_lo, y, core), pair: 8 (over z, x_hi).
Axes of the slice: x: 4 (x_hi: 2, x_lo: 2; x = x_hi * 2 + x_lo), y: 4, z: 4, core: 2. Of those that a mesh axis runs over, the one named last changes fastest.
Arguments:
- densities: bfloat16 [8192, 65536], P('comp', 'pair'), may hold values from -6 to 6
- coulomb: float32 [8192], replicated, may hold values from 3.314563e-05 to 0.003314563
- pair_list: int32 [1024, 2], P(('comp', 'pair')), may hold values from 0 to 4095
- valence_energy: float32 [4096], replicated, may hold values from -20 to -0.5, as said below
- conduction_energy: float32 [4096], replicated, may hold values from 0.5 to 12, as said below
- tile_mask: int32 [512, 16], P(('pair', 'comp')), may hold values 0 or 1
Outputs:
- kernel: float32 [65536, 1024], P(('pair', 'comp'))
Inputs may be any that keep to these rules, and one draw needn't show every extreme that they name: `valence_energy`: energies in electronvolts. `conduction_energy`: energies in electronvolts.
All inputs are finite; a program needn't handle non-finite values. No bound on the sum of `tile_mask` on one device may be relied on, other than what follows from the above.
Results may differ from a plain program's by a relative error of at most 0.0025.
Values may be sent and summed in bfloat16 or wider, within the bound.
No kernel may reach another device: no remote copies, remote signals or barrier semaphores. Data moves between devices by JAX's collectives and lax.ppermute only.
A program may use at most 128 MiB of HBM per device.

v0:
```python
import jax
import jax.numpy as jnp
from jax import lax
from jax.sharding import PartitionSpec as P

TILE = 128


def per_device(densities, coulomb, pair_list, valence_energy, conduction_energy, tile_mask):
    comp_count = lax.axis_size("comp")
    pair_count = lax.axis_size("pair")
    comp_index = lax.axis_index("comp")
    pair_index = lax.axis_index("pair")
    block_len = densities.shape[0]
    pair_dev = densities.shape[1] // comp_count
    row_dev = pair_list.shape[0]
    window = row_dev * comp_count * pair_count
    weights = lax.dynamic_slice_in_dim(coulomb, comp_index * block_len, block_len)
    picked = densities.reshape(block_len, comp_count, pair_dev)[:, :, :row_dev]
    local_panel = (jnp.transpose(picked, (1, 2, 0)).astype(jnp.float32) * weights).astype(
        jnp.bfloat16
    )
    gathered = lax.all_gather(local_panel, "pair", axis=1, tiled=True)
    panel = gathered.reshape(window, block_len)
    exchange = lax.psum_scatter(
        lax.dot_general(
            densities, panel, (((0,), (1,)), ((), ())), preferred_element_type=jnp.float32
        ),
        "comp",
        scatter_dimension=0,
        tiled=True,
    )
    masked = (
        exchange.reshape(pair_dev // TILE, TILE, comp_count, window // comp_count)
        * tile_mask.astype(jnp.float32)[:, None, :, None]
    )
    masked = 2.0 * masked.reshape(pair_dev, window)
    table = jnp.arange(valence_energy.shape[0], dtype=jnp.int32)
    cond_hits = pair_list[:, 1][:, None] == table[None, :]
    val_hits = pair_list[:, 0][:, None] == table[None, :]
    energy = jnp.sum(jnp.where(cond_hits, conduction_energy[None, :], 0.0), axis=1) - jnp.sum(
        jnp.where(val_hits, valence_energy[None, :], 0.0), axis=1
    )
    diag_block = jnp.eye(row_dev, dtype=jnp.float32) * energy[None, :]
    start = (comp_index * pair_count + pair_index) * row_dev
    placed = lax.dynamic_update_slice(
        jnp.zeros((pair_dev, window), jnp.float32), diag_block, (jnp.int32(0), start)
    )
    return masked + placed


def solution(mesh):
    return jax.shard_map(
        per_device,
        mesh=mesh,
        in_specs=(
            P("comp", "pair"),
            P(),
            P(("comp", "pair"), None),
            P(),
            P(),
            P(("pair", "comp"), None),
        ),
        out_specs=P(("pair", "comp"), None),
        check_vma=False,
    )
```

profile of v0, /device:TPU:0, one launch (start us, length us, event | category | flops | bytes accessed | tf_op | source)
XLA Modules:
  0.0 278.9 jit_solution(5608610415269672751)
XLA Ops:
  6.5 0.0 all-gather.2.cloned.1.call-start
  6.5 12.0 %copy.12 = bf16[512,8192]{0,1:T(8,128)(2,1)} copy(bf16[512,8192]{1,0:T(8,128)(2,1)} %param.6) | data formatting | bytes 16777216 | tf_op args[0]
  18.5 0.8 dynamic_slice.3
  19.3 1.6 fusion.1
  20.9 0.0 all-gather.2.cloned.1.call-update
  20.9 0.0 reduce-scatter.2.cloned.1.call-start
  20.9 48.0 %all-gather.2.cloned.1.call-done = bf16[16,64,512]{2,1,0:T(8,128)(2,1)} async-done(((bf16[16,8,512]{2,1,0:T(8,128)(2,1)}), bf16[16,64,512]{2,1,0:T(8,128)(2,1)}) %all-gather.2.cloned.1.call-update) | async-done | bytes 1048592 | tf_op jit(solution)/shard_map/all_gather | solution.py:23
  68.9 17.7 %convolution_bitcast_fusion = f32[8192,1024]{0,1:T(8,128)} fusion(bf16[1024,512]{1,0:T(8,128)(2,1)} %bitcast.22, bf16[512,8192]{1,0:T(8,128)(2,1)} %param.6), kind=kOutput, calls=%fused_computation | convolution fusion | flops 8589934592 | bytes 42991616 | tf_op jit(solution)/shard_map/dot_general | solution.py:26
  86.7 0.0 copy-start.3
  86.7 0.0 copy-start.2
  86.7 0.0 reduce-scatter.2.cloned.1.call-update
  86.7 0.6 copy-done.3
  87.4 0.1 copy.13
  87.5 0.0 copy-done.4
  87.5 0.0 copy-done.1
  87.5 0.0 copy-done.2
  87.5 0.2 select_reduce_fusion
  87.7 179.8 %reduce-scatter.2.cloned.1.call-done = f32[512,1024]{0,1:T(8,128)} async-done(((f32[8192,1024]{0,1:T(8,128)}), f32[512,1024]{0,1:T(8,128)}) %reduce-scatter.2.cloned.1.call-update) | async-done | bytes 2097168 | tf_op jit(solution)/shard_map/reduce_scatter | solution.py:25
  267.6 0.3 mul.48
  267.9 1.2 copy-done
  269.2 0.5 fusion
  269.7 0.1 select_add_fusion
  269.7 0.5 add.18
  270.2 1.8 copy.14
  (6 shorter events, 0.0 us)
Async XLA Ops:
  6.5 62.4 %all-gather.2.cloned.1.call-start = ((), (), s32[]{:S(2)}) async-start(), calls=%async_computation.1 | async-start | bytes 1179648 | tf_op jit(solution)/shard_map/all_gather | solution.py:23
  20.9 246.7 %reduce-scatter.2.cloned.1.call-start = ((), (), s32[]{:S(2)}) async-start(), calls=%async_computation.2 | async-start | bytes 35651584 | tf_op jit(solution)/shard_map/reduce_scatter | solution.py:25
  86.7 0.7 copy-start.3
  86.7 0.8 copy-start.4
  86.7 0.8 copy-start.1
  86.7 0.8 copy-start.2
  267.6 1.6 copy-start
Sparse Core Ops, SparseCore 0:
  21.0 47.8 all-gather.1
  86.9 180.6 reduce-scatter.1
where the time goes:
time: 279 us
  waiting for transfers between devices  228 us (82%)
  matrix products  17.7 us (6%)
  local copies, waits for them, and re-layouts  17.3 us (6%)
  between operations  13.5 us (5%)
    reduce_scatter x1, waiting for transfers between devices, per_device(): lax.psum_scatter(lax.dot_general(densities, panel, (((0,), (1,)), ((), ()...  180 us
    all_gather x1, waiting for transfers between devices, per_device(): gathered = lax.all_gather(local_panel, 'pair', axis=1, tiled=True)  48 us
    dot_general x1, matrix products, per_device(): lax.dot_general(densities, panel, (((0,), (1,)), ((), ())), preferred_ele...  17.7 us
    unnamed x11, local copies, waits for them, and re-layouts  13.9 us
  transfers between devices with their start and end apart: 2, of which 2 were waited for; matrix products, arithmetic and copies ran while one was open for 0% of the time, Pallas kernels for 0%

commit v1 on v0

--- a/solution.py
+++ b/solution.py
@@ -20,7 +20,9 @@
     local_panel = (jnp.transpose(picked, (1, 2, 0)).astype(jnp.float32) * weights).astype(
         jnp.bfloat16
     )
-    gathered = lax.all_gather(local_panel, "pair", axis=1, tiled=True)
+    gathered = jnp.concatenate(
+        lax.all_to_all(jnp.stack([local_panel] * lax.axis_size("pair")), "pair", 0, 0), axis=1
+    )
     panel = gathered.reshape(window, block_len)
     exchange = lax.psum_scatter(
         lax.dot_general(

time: 279 us -> 255 us (0.914)
  waiting for transfers between devices: 228 us -> 179 us
  blocking collectives: 0 us -> 24.9 us
    all_gather x1 -> x0, waiting for transfers between devices: 48 us -> none  [per_device(): gathered = lax.all_gather(local_panel, 'pair', axis=1, tiled=True)]
    all_to_all x0 -> x1, blocking collectives: none -> 24.9 us  [per_device(): lax.all_to_all(jnp.stack([local_panel] * lax.axis_size('pair')), 'pair',...]
    unnamed x11 -> x10, local copies, waits for them, and re-layouts: 13.9 us -> 1.9 us
    reshape x0 -> x1, local copies, waits for them, and re-layouts: none -> 12 us  [per_device(): picked = densities.reshape(block_len, comp_count, pair_dev)[:, :, :row_dev]]
  transfers between devices with their start and end apart: 2 -> 1, of which waited for: 2 -> 1; matrix products, arithmetic and copies ran while one was open for 0% -> 0% of each run, Pallas kernels for 0% -> 0%
where the time goes in v1:
time: 255 us
  waiting for transfers between devices  179 us (70%)
  blocking collectives  24.9 us (10%)
  matrix products  17.8 us (7%)
  local copies, waits for them, and re-layouts  17.5 us (7%)
  between operations  13.5 us (5%)
    reduce_scatter x1, waiting for transfers between devices, per_device(): lax.psum_scatter(lax.dot_general(densities, panel, (((0,), (1,)), ((), ()...  179 us
    all_to_all x1, blocking collectives, per_device(): lax.all_to_all(jnp.stack([local_panel] * lax.axis_size('pair')), 'pair',...  24.9 us
    dot_general x1, matrix products, per_device(): lax.dot_general(densities, panel, (((0,), (1,)), ((), ())), preferred_ele...  17.8 us
    reshape x1, local copies, waits for them, and re-layouts, per_device(): picked = densities.reshape(block_len, comp_count, pair_dev)[:, :, :row_dev]  12 us
  transfers between devices with their start and end apart: 1, of which 1 were waited for; matrix products, arithmetic and copies ran while one was open for 0% of the time, Pallas kernels for 0%

profile of v1, /device:TPU:0, one launch (start us, length us, event | category | flops | bytes accessed | tf_op | source)
XLA Modules:
  0.0 254.6 jit_solution(14417251003131686145)
XLA Ops:
  6.5 0.0 reduce-scatter.2.cloned.1.call-start
  6.5 12.0 %copy.21 = bf16[512,8192]{0,1:T(8,128)(2,1)} copy(bf16[512,8192]{1,0:T(8,128)(2,1)} %param.6) | data formatting | bytes 16777216 | tf_op jit(solution)/shard_map/reshape | solution.py:19
  18.5 0.8 dynamic_slice.3
  19.3 0.9 fusion.1
  20.2 0.1 stack.2
  20.3 24.9 %all_to_all.5 = bf16[8,16,8,512]{3,2,1,0:T(8,128)(2,1)S(1)} all-to-all(bf16[8,16,8,512]{3,2,1,0:T(8,128)(2,1)S(1)} %stack.2), channel_id=1, replica_groups=mesh['comp'=16,'pair'=8] {'pair'}, dimensions={0} | all-to-all | bytes 2097152 | tf_op jit(solution)/shard_map/all_to_all | solution.py:24
  45.1 0.1 copy.18
  45.2 17.8 %convolution_bitcast_fusion = f32[8192,1024]{0,1:T(8,128)} fusion(bf16[1024,512]{1,0:T(8,128)(2,1)S(1)} %bitcast.24, bf16[512,8192]{1,0:T(8,128)(2,1)} %param.6), kind=kOutput, calls=%fused_computation | convolution fusion | flops 8589934592 | bytes 42991616 | tf_op jit(solution)/shard_map/dot_general | solution.py:28
  63.1 0.0 copy-start.3
  63.1 0.0 copy-start.1
  63.1 0.0 reduce-scatter.2.cloned.1.call-update
  63.1 0.6 copy-done.3
  63.8 0.1 copy.19
  63.8 0.0 copy-done.4
  63.9 0.0 copy-done.1
  63.9 0.0 copy-done.2
  63.9 0.2 select_reduce_fusion
  64.1 179.1 %reduce-scatter.2.cloned.1.call-done = f32[512,1024]{0,1:T(8,128)} async-done(((f32[8192,1024]{0,1:T(8,128)}), f32[512,1024]{0,1:T(8,128)}) %reduce-scatter.2.cloned.1.call-update) | async-done | bytes 2097168 | tf_op jit(solution)/shard_map/reduce_scatter | solution.py:27
  243.3 0.3 mul.48
  243.6 1.2 copy-done
  244.9 0.5 fusion
  245.4 0.1 select_add_fusion
  245.4 0.5 add.18
  245.9 1.8 copy.20
  (6 shorter events, 0.0 us)
Async XLA Ops:
  6.5 236.7 %reduce-scatter.2.cloned.1.call-start = ((), (), s32[]{:S(2)}) async-start(), calls=%async_computation.2 | async-start | bytes 35651584 | tf_op jit(solution)/shard_map/reduce_scatter | solution.py:27
  63.1 0.7 copy-start.3
  63.1 0.8 copy-start.4
  63.1 0.8 copy-start.1
  63.1 0.8 copy-start.2
  243.3 1.6 copy-start
Sparse Core Ops, SparseCore 0:
  63.2 179.9 reduce-scatter.1
